TPU v7x, 512 devices: a whole 4x8x8 slice. The times are simulated.
512 devices in a mesh: rep: 4 (over x), node: 16 (over y, core), local: 8 (over z).
Axes of the slice: x: 4, y: 8, z: 8, core: 2. Of those that a mesh axis runs over, the one named last changes fastest.
Arguments:
- tokens: bfloat16 [8192, 4096], P(('rep', 'node', 'local')), may hold values from -6 to 6
- expert_ids: int32 [8192, 8], P(('rep', 'node', 'local')), may hold values from 0 to 127, all different within a row; in each aligned block of 16 rows (0 to 15, 16 to 31, ...) at most 2 rows name the same one
- route_weights: float32 [8192, 8], P(('rep', 'node', 'local')), may hold values from 0.1 to 1
- gate_weight: bfloat16 [128, 768, 4096], P(('node', 'local'), 'rep'), may hold values from -0.09375 to 0.09375
- up_weight: bfloat16 [128, 768, 4096], P(('node', 'local'), 'rep'), may hold values from -0.09375 to 0.09375
- down_weight: bfloat16 [128, 768, 4096], P(('node', 'local'), None, 'rep'), may hold values from -0.21875 to 0.21875
Outputs:
- mixed_rows: bfloat16 [8192, 4096], P(('rep', 'node', 'local'))
Inputs may be any that keep to these rules, and one draw needn't show every extreme that they name: `expert_ids`: each row names 8 different experts. Among the rows of one device (aligned blocks of 16 rows) no expert is named by more than 2 rows, and in some blocks some expert is named by exactly 2 rows.
All inputs are finite; a program needn't handle non-finite values.
Results may differ from a plain program's by a relative error of at most 0.0057.
Values may be sent and summed in bfloat16 or wider, within the bound.
A program may use at most 64 MiB of HBM per device.

v0:
```python
import jax
import jax.numpy as jnp
from jax import lax
from jax.sharding import PartitionSpec as P


def slot_table(expert_ids, expert_count, slot_cap):
    row_count, top_count = expert_ids.shape
    flat_ids = expert_ids.reshape(-1)
    same = flat_ids[:, None] == flat_ids[None, :]
    place = jnp.arange(row_count * top_count, dtype=jnp.int32)
    rank_of = jnp.sum((same & (place[None, :] < place[:, None])).astype(jnp.int32), axis=1)
    return (flat_ids * slot_cap + rank_of).reshape(row_count, top_count)


def route_slots(blocks):
    return lax.all_to_all(blocks, ("node", "local"), split_axis=1, concat_axis=1, tiled=True)


def on_device(tokens, expert_ids, route_weights, gate_weight, up_weight, down_weight):
    row_count, top_count = expert_ids.shape
    model_width = tokens.shape[1]
    node_count = lax.axis_size("node")
    plane_count = lax.axis_size("rep")
    expert_count = node_count * lax.axis_size("local")
    slot_cap = min(row_count, max(2, 2 * row_count * top_count // expert_count))
    slot_total = expert_count * slot_cap
    slot_of = slot_table(expert_ids, expert_count, slot_cap)
    slot_iota = jnp.arange(slot_total, dtype=jnp.int32)
    placed = jnp.any(slot_of[None, :, :] == slot_iota[:, None, None], axis=2).astype(jnp.bfloat16)
    outgoing = jnp.dot(placed, tokens, preferred_element_type=jnp.float32).astype(jnp.bfloat16)
    mixing = jnp.sum(
        jnp.where(slot_of[:, :, None] == slot_iota[None, None, :], route_weights[:, :, None], 0.0),
        axis=1,
    )
    arrived = route_slots(outgoing.reshape(1, expert_count, slot_cap, model_width))
    arrived = arrived.reshape(slot_total, model_width)
    gate_local = gate_weight[0]
    up_local = up_weight[0]
    down_local = down_weight[0]
    quarter_width = down_local.shape[1]
    feature_dims = (((1,), (1,)), ((), ()))
    shard_piece = lax.all_gather(arrived, "rep", axis=0, tiled=True)
    gate_part = lax.dot_general(
        shard_piece, gate_local, feature_dims, preferred_element_type=jnp.float32
    )
    up_part = lax.dot_general(
        shard_piece, up_local, feature_dims, preferred_element_type=jnp.float32
    )
    hidden_part = (jax.nn.silu(gate_part) * up_part).astype(jnp.bfloat16)
    expert_out = jnp.dot(
        lax.all_gather(hidden_part, "rep", axis=1, tiled=True),
        down_local,
        preferred_element_type=jnp.float32,
    ).astype(jnp.bfloat16)
    own_slots = lax.all_to_all(
        expert_out.reshape(plane_count, slot_total, quarter_width),
        "rep",
        split_axis=0,
        concat_axis=2,
        tiled=True,
    )
    returned = route_slots(own_slots.reshape(1, expert_count, slot_cap, model_width))
    back_rows = returned.reshape(slot_total, model_width).astype(jnp.float32)
    mixed_rows = jnp.dot(mixing, back_rows, precision=lax.Precision.HIGHEST)
    return mixed_rows.astype(jnp.bfloat16)


def solution(mesh):
    placed = (
        P(("rep", "node", "local"), None),
        P(("rep", "node", "local"), None),
        P(("rep", "node", "local"), None),
        P(("node", "local"), "rep", None),
        P(("node", "local"), "rep", None),
        P(("node", "local"), None, "rep"),
    )
    return jax.shard_map(
        on_device,
        mesh=mesh,
        in_specs=placed,
        out_specs=P(("rep", "node", "local"), None),
        check_vma=False,
    )
```

profile of v0, /device:TPU:1, one launch (start us, length us, event | category | flops | bytes accessed | tf_op | source)
XLA Modules:
  0.0 339.2 jit_solution(8202762404922500141)
XLA Ops:
  6.5 0.9 copy.20
  7.4 0.1 eq.20
  7.5 0.2 convert_reduce_fusion
  7.7 0.1 reduce_sum.21
  7.8 0.1 fusion.11
  7.9 3.0 convolution_convert_fusion
  10.9 4.4 %reshape.32 = bf16[1,128,2,4096]{3,2,1,0:T(2,128)(2,1)} reshape(bf16[256,4096]{1,0:T(8,128)(2,1)} %convolution_convert_fusion) | data formatting | bytes 4194304 | tf_op jit(solution)/shard_map/reshape | solution.py:36
  15.3 72.7 %all_to_all.25 = bf16[1,128,2,4096]{3,2,0,1:T(2,128)(2,1)} all-to-all(bf16[1,128,2,4096]{3,2,0,1:T(2,128)(2,1)} %bitcast.31), channel_id=1, replica_groups=mesh['rep'=4,'node'=16,'local'=8] {'node','local'}, dimensions={1} | all-to-all | bytes 4194304 | tf_op jit(solution)/shard_map/all_to_all | solution.py:17
  88.0 4.1 %reshape.33 = bf16[256,4096]{1,0:T(8,128)(2,1)} reshape(bf16[1,128,2,4096]{3,2,0,1:T(2,128)(2,1)} %all_to_all.25) | data formatting | bytes 4194304 | tf_op jit(solution)/shard_map/reshape | solution.py:37
  92.1 0.0 all-gather.5.cloned.1.call-start
  92.2 81.1 %all-gather.3.cloned.1.call-done = bf16[1024,4096]{1,0:T(8,128)(2,1)} async-done(((bf16[256,4096]{1,0:T(8,128)(2,1)}), bf16[1024,4096]{1,0:T(8,128)(2,1)}) %all-gather.3.cloned.1.call-update) | async-done | bytes 8388624 | tf_op jit(solution)/shard_map/all_gather | solution.py:43
  173.3 6.4 %fusion.3 = f32[1024,192]{0,1:T(8,128)S(1)} fusion(bf16[1024,4096]{1,0:T(8,128)(2,1)} %all-gather.3.cloned.1.call-done, bf16[1,192,4096]{2,1,0:T(8,128)(2,1)S(1)} %copy-done.3), kind=kOutput, calls=%fused_computation.6 | convolution fusion | flops 1610612736 | bytes 10747904 | tf_op jit(solution)/shard_map/dot_general | solution.py:44
  179.8 3.7 %fusion.8 = bf16[1024,192]{0,1:T(8,128)(2,1)} fusion(bf16[1024,4096]{1,0:T(8,128)(2,1)S(1)} %copy-done.2, bf16[1,192,4096]{2,1,0:T(8,128)(2,1)S(1)} %copy-done.4, f32[1024,192]{0,1:T(8,128)S(1)} %fusion.3), kind=kOutput, calls=%fused_computation.9 | convolution fusion | flops 1611792384 | bytes 11141120 | tf_op jit(solution)/shard_map/dot_general | solution.py:47
  183.5 33.0 %all-gather.5.cloned.1.call-done = bf16[1024,768]{0,1:T(8,128)(2,1)} async-done(((bf16[1024,192]{0,1:T(8,128)(2,1)}), bf16[1024,768]{0,1:T(8,128)(2,1)}) %all-gather.5.cloned.1.call-update) | async-done | bytes 1572880 | tf_op jit(solution)/shard_map/all_gather | solution.py:52
  216.5 3.2 convolution_convert_fusion.2
  219.7 27.8 %all_to_all.26 = bf16[4,256,1024]{2,1,0:T(8,128)(2,1)S(1)} all-to-all(bf16[4,256,1024]{2,1,0:T(8,128)(2,1)S(1)} %bitcast.33), channel_id=1, replica_groups=mesh['rep'=4,'node'=16,'local'=8] {'rep'}, dimensions={0} | all-to-all | bytes 4194304 | tf_op jit(solution)/shard_map/all_to_all | solution.py:56
  247.5 2.9 copy.24
  250.5 4.4 %reshape.35 = bf16[1,128,2,4096]{3,2,1,0:T(2,128)(2,1)} reshape(bf16[1,256,4,1024]{3,2,1,0:T(4,128)(2,1)} %copy.24) | data formatting | bytes 4194304 | tf_op jit(solution)/shard_map/reshape | solution.py:63
  254.8 16.4 %all-to-all-start.2 = ((bf16[1,128,2,4096]{3,2,0,1:T(2,128)(2,1)}), bf16[1,128,2,4096]{3,2,0,1:T(2,128)(2,1)}, u32[]{:S(2)}, u32[]{:S(2)}) async-start(bf16[1,128,2,4096]{3,2,0,1:T(2,128)(2,1)} %bitcast.30), calls=%async_computation.2 | async-start | bytes 4194304 | tf_op jit(solution)/shard_map/all_to_all | solution.py:17
  271.2 0.1 copy.22
  271.3 0.1 select_reduce_fusion
  271.4 53.6 %all-to-all-done.2 = bf16[1,128,2,4096]{3,2,0,1:T(2,128)(2,1)} async-done(((bf16[1,128,2,4096]{3,2,0,1:T(2,128)(2,1)}), bf16[1,128,2,4096]{3,2,0,1:T(2,128)(2,1)}, u32[]{:S(2)}, u32[]{:S(2)}) %all-to-all-start.2) | async-done | bytes 2097184 | tf_op jit(solution)/shard_map/all_to_all | solution.py:17
  325.0 4.1 %reshape.36 = bf16[256,4096]{1,0:T(8,128)(2,1)} reshape(bf16[1,128,2,4096]{3,2,0,1:T(2,128)(2,1)} %all-to-all-done.2) | data formatting | bytes 4194304 | tf_op jit(solution)/shard_map/reshape | solution.py:64
  329.1 3.2 convolution_convert_fusion.1
  (14 shorter events, 0.1 us)
Async XLA Ops:
  6.5 210.0 %copy-start = (bf16[1,768,1024]{2,1,0:T(8,128)(2,1)S(1)}, bf16[1,768,1024]{2,1,0:T(8,128)(2,1)}, u32[]{:S(2)}) copy-start(bf16[1,768,1024]{2,1,0:T(8,128)(2,1)} %param.11) | copy-start | bytes 4718596
  6.5 166.8 %all-gather.3.cloned.1.call-start = ((), (), s32[]{:S(2)}) async-start(), calls=%async_computation.3 | async-start | bytes 10485760 | tf_op jit(solution)/shard_map/all_gather | solution.py:43
  92.1 81.2 %copy-start.3 = (bf16[1,192,4096]{2,1,0:T(8,128)(2,1)S(1)}, bf16[1,192,4096]{2,1,0:T(8,128)(2,1)}, u32[]{:S(2)}) copy-start(bf16[1,192,4096]{2,1,0:T(8,128)(2,1)} %param.9) | copy-start | bytes 4718596
  92.1 124.4 %all-gather.5.cloned.1.call-start = ((), (), s32[]{:S(2)}) async-start(), calls=%async_computation.4 | async-start | bytes 1966080 | tf_op jit(solution)/shard_map/all_gather | solution.py:52
  173.3 6.4 %copy-start.2 = (bf16[1024,4096]{1,0:T(8,128)(2,1)S(1)}, bf16[1024,4096]{1,0:T(8,128)(2,1)}, u32[]{:S(2)}) copy-start(bf16[1024,4096]{1,0:T(8,128)(2,1)} %all-gather.3.cloned.1.call-done) | copy-start | bytes 25165828
  173.3 6.4 %copy-start.4 = (bf16[1,192,4096]{2,1,0:T(8,128)(2,1)S(1)}, bf16[1,192,4096]{2,1,0:T(8,128)(2,1)}, u32[]{:S(2)}) copy-start(bf16[1,192,4096]{2,1,0:T(8,128)(2,1)} %param.10) | copy-start | bytes 4718596
  254.8 16.4 %copy-start.1 = (f32[16,8]{0,1:T(8,128)S(1)}, f32[16,8]{0,1:T(8,128)}, u32[]{:S(2)}) copy-start(f32[16,8]{0,1:T(8,128)} %param.8) | copy-start | bytes 1540
  254.8 70.2 %all-to-all-start.2 = ((bf16[1,128,2,4096]{3,2,0,1:T(2,128)(2,1)}), bf16[1,128,2,4096]{3,2,0,1:T(2,128)(2,1)}, u32[]{:S(2)}, u32[]{:S(2)}) async-start(bf16[1,128,2,4096]{3,2,0,1:T(2,128)(2,1)} %bitcast.30), calls=%async_computation.2 | async-start | bytes 4194304 | tf_op jit(solution)/shard_map/all_to_all | solution.py:17
Sparse Core Ops, SparseCore 0:
  92.3 80.9 all-gather.2
  183.6 32.8 all-gather.4
where the time goes:
time: 340 us; the launch traced here: 339 us
  waiting for transfers between devices  168 us (49%)
  blocking collectives  100 us (29%)
  local copies, waits for them, and re-layouts  21.1 us (6%)
  matrix products  19.5 us (6%)
  starting transfers between devices  16.4 us (5%)
  between operations  13.5 us (4%)
    all_gather x1, waiting for transfers between devices, on_device(): shard_piece = lax.all_gather(arrived, 'rep', axis=0, tiled=True)  81.1 us
    all_to_all x1, blocking collectives, route_slots(): lax.all_to_all(blocks, ('node', 'local'), split_axis=1, concat_axis=1, ti...  72.7 us
    all_to_all x1, waiting for transfers between devices, route_slots(): lax.all_to_all(blocks, ('node', 'local'), split_axis=1, concat_axis=1, ti...  53.6 us
    all_gather x1, waiting for transfers between devices, on_device(): lax.all_gather(hidden_part, 'rep', axis=1, tiled=True)  33 us
    all_to_all x1, blocking collectives, on_device(): lax.all_to_all(expert_out.reshape(plane_count, slot_total, quarter_width)...  27.8 us
    all_to_all x1, starting transfers between devices, route_slots(): lax.all_to_all(blocks, ('node', 'local'), split_axis=1, concat_axis=1, ti...  16.4 us
  transfers between devices with their start and end apart: 3, of which 3 were waited for; matrix products, arithmetic and copies ran while one was open for 0% of the time, Pallas kernels for 0%

commit v1 on v0

--- a/solution.py
+++ b/solution.py
@@ -40,7 +40,12 @@
     down_local = down_weight[0]
     quarter_width = down_local.shape[1]
     feature_dims = (((1,), (1,)), ((), ()))
-    shard_piece = lax.all_gather(arrived, "rep", axis=0, tiled=True)
+    ring = [arrived]
+    for hop in range(3):
+        ring.append(lax.ppermute(ring[-1], "rep", [(dev, (dev + 1) % 4) for dev in range(4)]))
+    shard_piece = jnp.roll(
+        jnp.concatenate(ring[::-1], axis=0), (lax.axis_index("rep") + 1) * ring[0].shape[0], axis=0
+    )
     gate_part = lax.dot_general(
         shard_piece, gate_local, feature_dims, preferred_element_type=jnp.float32
     )

time: 340 us -> 408 us (1.20)
  waiting for transfers between devices: 168 us -> 220 us
  local copies, waits for them, and re-layouts: 21.1 us -> 33.3 us
  starting transfers between devices: 16.4 us -> 23.1 us
    ppermute x0 -> x3, waiting for transfers between devices: none -> 143 us  [on_device(): lax.ppermute(ring[-1], 'rep', [(dev, (dev + 1) % 4) for dev in range(4)])]
    all_gather x1 -> x0, waiting for transfers between devices: 81.1 us -> none  [on_device(): shard_piece = lax.all_gather(arrived, 'rep', axis=0, tiled=True)]
    unnamed x12 -> x23, local copies, waits for them, and re-layouts: 0.97 us -> 13 us
    all_gather x1, waiting for transfers between devices: 33 us -> 23.1 us  [on_device(): lax.all_gather(hidden_part, 'rep', axis=1, tiled=True)]
    ppermute x0 -> x3, starting transfers between devices: none -> 6.93 us  [on_device(): lax.ppermute(ring[-1], 'rep', [(dev, (dev + 1) % 4) for dev in range(4)])]
  transfers between devices with their start and end apart: 3 -> 5, of which waited for: 3 -> 5; matrix products, arithmetic and copies ran while one was open for 0% -> 0% of each run, Pallas kernels for 0% -> 0%
where the time goes in v1:
time: 408 us; the launch traced here: 407 us
  waiting for transfers between devices  220 us (54%)
  blocking collectives  100 us (25%)
  local copies, waits for them, and re-layouts  33.3 us (8%)
  starting transfers between devices  23.1 us (6%)
  matrix products  16 us (4%)
  between operations  13.6 us (3%)
    ppermute x3, waiting for transfers between devices, on_device(): lax.ppermute(ring[-1], 'rep', [(dev, (dev + 1) % 4) for dev in range(4)])  143 us
    all_to_all x1, blocking collectives, route_slots(): lax.all_to_all(blocks, ('node', 'local'), split_axis=1, concat_axis=1, ti...  72.7 us
    all_to_all x1, waiting for transfers between devices, route_slots(): lax.all_to_all(blocks, ('node', 'local'), split_axis=1, concat_axis=1, ti...  53.6 us
    all_to_all x1, blocking collectives, on_device(): lax.all_to_all(expert_out.reshape(plane_count, slot_total, quarter_width)...  27.8 us
    all_gather x1, waiting for transfers between devices, on_device(): lax.all_gather(hidden_part, 'rep', axis=1, tiled=True)  23.1 us
    all_to_all x1, starting transfers between devices, route_slots(): lax.all_to_all(blocks, ('node', 'local'), split_axis=1, concat_axis=1, ti...  16.2 us
    unnamed x23, local copies, waits for them, and re-layouts  13 us
  transfers between devices with their start and end apart: 5, of which 5 were waited for; matrix products, arithmetic and copies ran while one was open for 0% of the time, Pallas kernels for 0%

profile of v1, /device:TPU:1, one launch (start us, length us, event | category | flops | bytes accessed | tf_op | source)
XLA Modules:
  0.0 406.6 jit_solution(17854523372832365783)
XLA Ops:
  7.9 3.0 convolution_convert_fusion
  10.9 4.4 %reshape.32 = bf16[1,128,2,4096]{3,2,1,0:T(2,128)(2,1)} reshape(bf16[256,4096]{1,0:T(8,128)(2,1)} %convolution_convert_fusion) | data formatting | bytes 4194304 | tf_op jit(solution)/shard_map/reshape | solution.py:36
  15.3 72.7 %all_to_all.25 = bf16[1,128,2,4096]{3,2,0,1:T(2,128)(2,1)} all-to-all(bf16[1,128,2,4096]{3,2,0,1:T(2,128)(2,1)} %bitcast.27), channel_id=1, replica_groups=mesh['rep'=4,'node'=16,'local'=8] {'node','local'}, dimensions={1} | all-to-all | bytes 4194304 | tf_op jit(solution)/shard_map/all_to_all | solution.py:17
  88.0 4.1 %reshape.33 = bf16[256,4096]{1,0:T(8,128)(2,1)} reshape(bf16[1,128,2,4096]{3,2,0,1:T(2,128)(2,1)} %all_to_all.25) | data formatting | bytes 4194304 | tf_op jit(solution)/shard_map/reshape | solution.py:37
  92.1 3.1 collective-permute-start
  95.2 47.0 %collective-permute-done = bf16[256,4096]{1,0:T(8,128)(2,1)S(1)} collective-permute-done((bf16[256,4096]{1,0:T(8,128)(2,1)}, bf16[256,4096]{1,0:T(8,128)(2,1)S(1)}, u32[]{:S(2)}, u32[]{:S(2)}) %collective-permute-start) | collective-permute-done | bytes 2097184 | tf_op jit(solution)/shard_map/ppermute | solution.py:45
  143.5 1.9 collective-permute-start.1
  145.5 48.3 %collective-permute-done.1 = bf16[256,4096]{1,0:T(8,128)(2,1)} collective-permute-done((bf16[256,4096]{1,0:T(8,128)(2,1)S(1)}, bf16[256,4096]{1,0:T(8,128)(2,1)}, u32[]{:S(2)}, u32[]{:S(2)}) %collective-permute-start.1) | collective-permute-done | bytes 2097184 | tf_op jit(solution)/shard_map/ppermute | solution.py:45
  193.8 1.9 collective-permute-start.2
  195.7 47.6 %collective-permute-done.2 = bf16[256,4096]{1,0:T(8,128)(2,1)} collective-permute-done((bf16[256,4096]{1,0:T(8,128)(2,1)}, bf16[256,4096]{1,0:T(8,128)(2,1)}, u32[]{:S(2)}, u32[]{:S(2)}) %collective-permute-start.2) | collective-permute-done | bytes 2097184 | tf_op jit(solution)/shard_map/ppermute | solution.py:45
  245.1 1.9 constant_dynamic-update-slice_fusion.6
  249.1 1.8 constant_dynamic-update-slice_fusion.3
  250.9 1.8 constant_dynamic-update-slice_fusion.2
  254.3 2.9 fusion.2
  257.2 3.7 multiply_convert_fusion
  260.9 23.1 %all-gather.2.cloned.1.call-done = bf16[1024,768]{0,1:T(8,128)(2,1)} async-done(((bf16[1024,192]{0,1:T(8,128)(2,1)}), bf16[1024,768]{0,1:T(8,128)(2,1)}) %all-gather.2.cloned.1.call-update) | async-done | bytes 1572880 | tf_op jit(solution)/shard_map/all_gather | solution.py:57
  284.0 3.2 convolution_convert_fusion.2
  287.3 27.8 %all_to_all.26 = bf16[4,256,1024]{2,1,0:T(8,128)(2,1)S(1)} all-to-all(bf16[4,256,1024]{2,1,0:T(8,128)(2,1)S(1)} %bitcast.29), channel_id=1, replica_groups=mesh['rep'=4,'node'=16,'local'=8] {'rep'}, dimensions={0} | all-to-all | bytes 4194304 | tf_op jit(solution)/shard_map/all_to_all | solution.py:61
  315.0 3.0 copy.24
  318.0 4.4 %reshape.35 = bf16[1,128,2,4096]{3,2,1,0:T(2,128)(2,1)} reshape(bf16[1,256,4,1024]{3,2,1,0:T(4,128)(2,1)} %copy.24) | data formatting | bytes 4194304 | tf_op jit(solution)/shard_map/reshape | solution.py:68
  322.4 16.2 %all-to-all-start.2 = ((bf16[1,128,2,4096]{3,2,0,1:T(2,128)(2,1)}), bf16[1,128,2,4096]{3,2,0,1:T(2,128)(2,1)}, u32[]{:S(2)}, u32[]{:S(2)}) async-start(bf16[1,128,2,4096]{3,2,0,1:T(2,128)(2,1)} %bitcast.26), calls=%async_computation.2 | async-start | bytes 4194304 | tf_op jit(solution)/shard_map/all_to_all | solution.py:17
  338.8 53.6 %all-to-all-done.2 = bf16[1,128,2,4096]{3,2,0,1:T(2,128)(2,1)} async-done(((bf16[1,128,2,4096]{3,2,0,1:T(2,128)(2,1)}), bf16[1,128,2,4096]{3,2,0,1:T(2,128)(2,1)}, u32[]{:S(2)}, u32[]{:S(2)}) %all-to-all-start.2) | async-done | bytes 2097184 | tf_op jit(solution)/shard_map/all_to_all | solution.py:17
  392.4 4.1 %reshape.36 = bf16[256,4096]{1,0:T(8,128)(2,1)} reshape(bf16[1,128,2,4096]{3,2,0,1:T(2,128)(2,1)} %all-to-all-done.2) | data formatting | bytes 4194304 | tf_op jit(solution)/shard_map/reshape | solution.py:69
  396.5 3.2 convolution_convert_fusion.1
  (29 shorter events, 8.2 us)
Async XLA Ops:
  6.5 277.5 %copy-start = (bf16[1,768,1024]{2,1,0:T(8,128)(2,1)S(1)}, bf16[1,768,1024]{2,1,0:T(8,128)(2,1)}, u32[]{:S(2)}) copy-start(bf16[1,768,1024]{2,1,0:T(8,128)(2,1)} %param.11) | copy-start | bytes 4718596
  6.5 277.5 %all-gather.2.cloned.1.call-start = ((), (), s32[]{:S(2)}) async-start(), calls=%async_computation.3 | async-start | bytes 1966080 | tf_op jit(solution)/shard_map/all_gather | solution.py:57
  92.1 50.1 %collective-permute-start = (bf16[256,4096]{1,0:T(8,128)(2,1)}, bf16[256,4096]{1,0:T(8,128)(2,1)S(1)}, u32[]{:S(2)}, u32[]{:S(2)}) collective-permute-start(bf16[256,4096]{1,0:T(8,128)(2,1)} %reshape.33), channel_id=1, source_target_pairs={{0,128},{128,256},{256,384},{384,0},{1,129},{129,257},{257,385},{3... | collective-permute-start | bytes 6291464 | tf_op jit(solution)/shard_map/ppermute | solution.py:45
  142.2 1.3 copy-start.2
  143.5 50.2 %collective-permute-start.1 = (bf16[256,4096]{1,0:T(8,128)(2,1)S(1)}, bf16[256,4096]{1,0:T(8,128)(2,1)}, u32[]{:S(2)}, u32[]{:S(2)}) collective-permute-start(bf16[256,4096]{1,0:T(8,128)(2,1)S(1)} %collective-permute-done), channel_id=1, source_target_pairs={{0,128},{128,256},{256,384},{384,0},{1,129},{129,257},{257,385},{3... | collective-permute-start | bytes 6291464 | tf_op jit(solution)/shard_map/ppermute | solution.py:45
  193.8 49.5 %collective-permute-start.2 = (bf16[256,4096]{1,0:T(8,128)(2,1)}, bf16[256,4096]{1,0:T(8,128)(2,1)}, u32[]{:S(2)}, u32[]{:S(2)}) collective-permute-start(bf16[256,4096]{1,0:T(8,128)(2,1)} %collective-permute-done.1), channel_id=1, source_target_pairs={{0,128},{128,256},{256,384},{384,0},{1,129},{129,257},{257,385},{3... | collective-permute-start | bytes 6291464 | tf_op jit(solution)/shard_map/ppermute | solution.py:45
  245.1 2.2 copy-start.3
  247.4 1.6 copy-start.1
  252.8 1.4 copy-start.5
  254.3 2.9 copy-start.6
  322.4 16.2 %copy-start.4 = (f32[16,8]{0,1:T(8,128)S(1)}, f32[16,8]{0,1:T(8,128)}, u32[]{:S(2)}) copy-start(f32[16,8]{0,1:T(8,128)} %param.8) | copy-start | bytes 1540
  322.4 70.0 %all-to-all-start.2 = ((bf16[1,128,2,4096]{3,2,0,1:T(2,128)(2,1)}), bf16[1,128,2,4096]{3,2,0,1:T(2,128)(2,1)}, u32[]{:S(2)}, u32[]{:S(2)}) async-start(bf16[1,128,2,4096]{3,2,0,1:T(2,128)(2,1)} %bitcast.26), calls=%async_computation.2 | async-start | bytes 4194304 | tf_op jit(solution)/shard_map/all_to_all | solution.py:17
Sparse Core Ops, SparseCore 0:
  261.1 22.9 all-gather.1
